TPU v7x, 512 devices: a whole 4x8x8 slice. The times are simulated.
512 devices in a mesh: gx: 8 (over y), gy: 4 (over x), gz: 16 (over z, core).
Axes of the slice: x: 4, y: 8, z: 8, core: 2. Of those that a mesh axis runs over, the one named last changes fastest.
Arguments:
- fields: float32 [4, 512, 256, 512], P(None, 'gz', 'gx', 'gy'), may hold values from -6 to 6
- material: int32 [512, 256, 512], P('gz', 'gx', 'gy'), may hold values from 0 to 15
- depth_order: int32 [16], replicated, may hold values from 0 to 15, each once
- table: float32 [4, 16], replicated, may hold values from 0.2 to 2
Outputs:
- image: float32 [4, 256, 512], P(None, ('gx', 'gz'), 'gy')
Inputs may be any that keep to these rules, and one draw needn't show every extreme that they name: `depth_order`: a permutation: each brick layer along gz gets a distinct rank, 0 nearest the viewer.
All inputs are finite; a program needn't handle non-finite values.
Results may differ from a plain program's by a relative error of at most 0.0003.
Values sent between devices are 32-bit elements; how exact they have to be, the bound alone decides.
A program may use at most 64 MiB of HBM per device.

v0:
```python
import jax
import jax.numpy as jnp
from jax import lax
from jax.sharding import PartitionSpec as P

ambient = 0.3
diffuse = 1.2
grad_floor = 0.0025
light_z = 2.0 / 3.0
light_x = 1.0 / 3.0
light_y = 2.0 / 3.0


def extended(cells, sides, width):
    for axis, dim in sides:
        count = lax.axis_size(axis)
        ends = count - 1
        head = lax.slice_in_dim(cells, 0, width, axis=dim)
        tail = lax.slice_in_dim(cells, cells.shape[dim] - width, cells.shape[dim], axis=dim)
        cells = jnp.concatenate(
            [
                lax.ppermute(tail, axis, [(i, (i + 1) % count) for i in range(ends)]),
                cells,
                lax.ppermute(head, axis, [((i + 1) % count, i) for i in range(ends)]),
            ],
            axis=dim,
        )
    return cells


def blur_axis(values, which):
    length = values.shape[which]
    lower = lax.slice_in_dim(values, 0, length - 2, axis=which)
    middle = lax.slice_in_dim(values, 1, length - 1, axis=which)
    upper = lax.slice_in_dim(values, 2, length, axis=which)
    return (lower + 2.0 * middle + upper) * 0.25


def slope_axis(values, which):
    length = values.shape[which]
    lower = lax.slice_in_dim(values, 0, length - 2, axis=which)
    upper = lax.slice_in_dim(values, 2, length, axis=which)
    return (upper - lower) * 0.5


def smooth_all(values):
    for which in (1, 2, 3):
        values = blur_axis(values, which)
    return values


def shade_brick(smoothed, density, material, table, depth_total):
    grad_z = blur_axis(blur_axis(slope_axis(density, 0), 1), 2)
    grad_x = blur_axis(blur_axis(slope_axis(density, 1), 0), 2)
    grad_y = blur_axis(blur_axis(slope_axis(density, 2), 0), 1)
    facing = jnp.abs(light_z * grad_z + light_x * grad_x + light_y * grad_y)
    length = jnp.sqrt(grad_z * grad_z + grad_x * grad_x + grad_y * grad_y + grad_floor)
    shading = ambient + diffuse * facing / length
    entries = table.shape[1]
    onehot = (material[None] == jnp.arange(entries, dtype=jnp.int32)[:, None, None, None]).astype(
        jnp.float32
    )
    looked = jnp.einsum("cm,mzxy->czxy", table, onehot, precision=lax.Precision.HIGHEST)
    extinct = looked[3] * jax.nn.softplus(3.0 * smoothed[0]) * (2.0 / depth_total)
    colour = looked[:3] * shading[None] * (0.5 + jax.nn.sigmoid(2.0 * smoothed[1:]))
    ahead = jnp.cumsum(extinct, axis=0) - extinct
    weight = jnp.exp(-ahead) * -jnp.expm1(-extinct)
    return (jnp.sum(weight[None] * colour, axis=1), jnp.sum(extinct, axis=0))


def on_device(fields, material, depth_order, table):
    zsize = fields.shape[1]
    xsize = fields.shape[2]
    ysize = fields.shape[3]
    layers = lax.axis_size("gz")
    depth_total = zsize * layers
    width_total = xsize * lax.axis_size("gx")
    height_total = ysize * lax.axis_size("gy")
    padded = extended(fields, (("gx", 2), ("gy", 3), ("gz", 1)), 2)
    smoothed = smooth_all(padded)
    zpos = lax.axis_index("gz") * zsize - 1 + jnp.arange(zsize + 2, dtype=jnp.int32)
    xpos = lax.axis_index("gx") * xsize - 1 + jnp.arange(xsize + 2, dtype=jnp.int32)
    ypos = lax.axis_index("gy") * ysize - 1 + jnp.arange(ysize + 2, dtype=jnp.int32)
    inside = (
        ((zpos >= 0) & (zpos < depth_total))[:, None, None]
        & ((xpos >= 0) & (xpos < width_total))[None, :, None]
        & ((ypos >= 0) & (ypos < height_total))[None, None, :]
    )
    density = jnp.where(inside, smoothed[0], jnp.zeros_like(smoothed[0]))
    inner = smoothed[:, 1:-1, 1:-1, 1:-1]
    colour, depth = shade_brick(inner, density, material, table, depth_total)
    rows = xsize // layers
    layer_index = lax.axis_index("gz")
    depths = lax.all_gather(depth[None], "gz", axis=0, tiled=True)
    own_rank = depth_order[layer_index]
    nearer = (depth_order < own_rank).astype(jnp.float32)
    atten = jnp.einsum("g,gxy->xy", nearer, depths, precision=lax.Precision.HIGHEST)
    blended = lax.psum_scatter(
        colour * jnp.exp(-atten)[None], "gz", scatter_dimension=1, tiled=True
    )
    total = lax.dynamic_slice_in_dim(jnp.sum(depths, axis=0), layer_index * rows, rows, 0)
    return jnp.concatenate([blended, (-jnp.expm1(-total))[None]], axis=0)


def solution(mesh):
    return jax.shard_map(
        on_device,
        mesh=mesh,
        in_specs=(P(None, "gz", "gx", "gy"), P("gz", "gx", "gy"), P(), P()),
        out_specs=P(None, ("gx", "gz"), "gy"),
        check_vma=False,
    )
```

profile of v0, /device:TPU:28, one launch (start us, length us, event | category | flops | bytes accessed | tf_op | source)
XLA Modules:
  0.0 145.0 jit_solution(10533029868132336585)
XLA Ops:
  0.0 0.0 copy-start
  0.0 1.3 fusion.63
  1.3 4.7 %collective-permute-start = (f32[4,32,2,128]{3,2,1,0:T(2,128)S(1)}, f32[4,32,2,128]{3,2,1,0:T(2,128)S(1)}, u32[]{:S(2)}, u32[]{:S(2)}) collective-permute-start(f32[4,32,2,128]{3,2,1,0:T(2,128)S(1)} %get-tuple-element.9), channel_id=1, source_target_pairs={{0,64},{64,128},{128,192},{192,256},{256,320},{320,384},{384,448},... | collective-permute-start | bytes 393224 | tf_op jit(solution)/shard_map/ppermute | solution.py:22
  6.0 1.9 %collective-permute-start.1 = (f32[4,32,2,128]{3,2,1,0:T(2,128)S(1)}, f32[4,32,2,128]{3,2,1,0:T(2,128)S(1)}, u32[]{:S(2)}, u32[]{:S(2)}) collective-permute-start(f32[4,32,2,128]{3,2,1,0:T(2,128)S(1)} %get-tuple-element.10), channel_id=1, source_target_pairs={{64,0},{128,64},{192,128},{256,192},{320,256},{384,320},{448,384},... | collective-permute-start | bytes 393224 | tf_op jit(solution)/shard_map/ppermute | solution.py:24
  8.0 4.5 %fusion = f32[32,32,128,4]{2,3,1,0:T(4,128)} fusion(s32[32,32,128]{2,1,0:T(8,128)} %param.5, f32[4,16]{1,0:T(4,128)S(1)} %copy-done), kind=kOutput, calls=%fused_computation.1 | convolution fusion | flops 102760448 | bytes 2621696 | tf_op jit(solution)/shard_map/cm,mzxy->czxy/dot_general | solution.py:63
  12.5 0.0 collective-permute-done
  12.5 1.6 %collective-permute-done.1 = f32[4,32,2,128]{3,2,1,0:T(2,128)S(1)} collective-permute-done((f32[4,32,2,128]{3,2,1,0:T(2,128)S(1)}, f32[4,32,2,128]{3,2,1,0:T(2,128)S(1)}, u32[]{:S(2)}, u32[]{:S(2)}) %collective-permute-start.1) | collective-permute-done | bytes 131104 | tf_op jit(solution)/shard_map/ppermute | solution.py:24
  14.1 1.9 %pad_maximum_fusion.6 = f32[4,32,36,128]{3,2,1,0:T(8,128)S(1)} fusion(f32[4,32,2,128]{3,2,1,0:T(2,128)S(1)} %collective-permute-done.1, f32[4,32,32,128]{3,2,1,0:T(8,128)} %param.4, f32[4,32,2,128]{3,2,1,0:T(2,128)S(1)} %collective-permute-done), kind=kLoop, calls=%fused_computation.21 | loop fusion | flops 1179648 | bytes 4718592 | tf_op jit(solution)/shard_map/concatenate | solution.py:20
  16.0 2.3 %fusion.62 = (f32[4,32,36,2]{3,2,1,0:T(8,128)}, f32[4,32,36,2]{3,2,1,0:T(8,128)S(1)}) fusion(f32[4,32,36,128]{3,2,1,0:T(8,128)S(1)} %pad_maximum_fusion.6), kind=kLoop, calls=%fused_computation.114 | loop fusion | bytes 147456 | tf_op jit(solution)/shard_map/slice | solution.py:19
  18.4 2.7 %copy.43 = f32[4,32,36,2]{2,1,3,0:T(8,128)S(1)} copy(f32[4,32,36,2]{3,2,1,0:T(8,128)} %get-tuple-element.7) | data formatting | bytes 73728 | tf_op jit(solution)/shard_map/slice | solution.py:19
  21.1 3.1 %collective-permute-start.2 = (f32[4,32,36,2]{2,1,3,0:T(8,128)S(1)}, f32[4,32,36,2]{2,1,3,0:T(8,128)S(1)}, u32[]{:S(2)}, u32[]{:S(2)}) collective-permute-start(f32[4,32,36,2]{2,1,3,0:T(8,128)S(1)} %copy.43), channel_id=1, source_target_pairs={{0,16},{16,32},{32,48},{1,17},{17,33},{33,49},{2,18},{18,34},{34,5... | collective-permute-start | bytes 110600 | tf_op jit(solution)/shard_map/ppermute | solution.py:22
  24.2 1.0 copy.44
  25.3 2.7 %collective-permute-start.3 = (f32[4,32,36,2]{2,1,3,0:T(8,128)S(1)}, f32[4,32,36,2]{2,1,3,0:T(8,128)S(1)}, u32[]{:S(2)}, u32[]{:S(2)}) collective-permute-start(f32[4,32,36,2]{2,1,3,0:T(8,128)S(1)} %copy.44), channel_id=1, source_target_pairs={{16,0},{32,16},{48,32},{17,1},{33,17},{49,33},{18,2},{34,18},{50,3... | collective-permute-start | bytes 110600 | tf_op jit(solution)/shard_map/ppermute | solution.py:24
  28.0 0.5 compare_and_fusion.1
  28.5 0.0 collective-permute-done.2
  28.5 1.0 copy.45
  29.5 2.6 %collective-permute-done.3 = f32[4,32,36,2]{2,1,3,0:T(8,128)S(1)} collective-permute-done((f32[4,32,36,2]{2,1,3,0:T(8,128)S(1)}, f32[4,32,36,2]{2,1,3,0:T(8,128)S(1)}, u32[]{:S(2)}, u32[]{:S(2)}) %collective-permute-start.3) | collective-permute-done | bytes 36896 | tf_op jit(solution)/shard_map/ppermute | solution.py:24
  32.1 2.5 %copy.46 = f32[4,32,36,2]{3,2,1,0:T(8,128)} copy(f32[4,32,36,2]{2,1,3,0:T(8,128)S(1)} %collective-permute-done.3) | data formatting | bytes 73728 | tf_op jit(solution)/shard_map/ppermute | solution.py:24
  34.6 1.5 %pad_maximum_fusion.11 = (f32[4,2,36,132]{3,2,1,0:T(8,128)S(1)}, f32[4,2,36,132]{3,2,1,0:T(8,128)S(1)}) fusion(f32[4,32,36,2]{3,2,1,0:T(8,128)} %copy.46, f32[4,32,36,2]{3,2,1,0:T(8,128)S(1)} %copy.45, f32[4,32,2,128]{3,2,1,0:T(2,128)S(1)} %collective-permute-done.1, f32[4,32,32,128]{3,2,1,0:T(8,128)} %param.4, f32[4,32,2,128]{3,2,1,0:T(2,128)S(1)} %collective-permute-done), kind=kLoop, calls=%fused_computation.92 | loop fusion | flops 304128 | bytes 2737152 | tf_op jit(solution)/shard_map/slice | solution.py:19
  36.2 2.0 %collective-permute-start.4 = (f32[4,2,36,132]{3,2,1,0:T(8,128)S(1)}, f32[4,2,36,132]{3,2,1,0:T(8,128)}, u32[]{:S(2)}, u32[]{:S(2)}) collective-permute-start(f32[4,2,36,132]{3,2,1,0:T(8,128)S(1)} %get-tuple-element.5), channel_id=1, source_target_pairs={{0,1},{1,2},{2,3},{3,4},{4,5},{5,6},{6,7},{7,8},{8,9},{9,10},{10,1... | collective-permute-start | bytes 456200 | tf_op jit(solution)/shard_map/ppermute | solution.py:22
  38.2 1.5 %collective-permute-start.5 = (f32[4,2,36,132]{3,2,1,0:T(8,128)S(1)}, f32[4,2,36,132]{3,2,1,0:T(8,128)}, u32[]{:S(2)}, u32[]{:S(2)}) collective-permute-start(f32[4,2,36,132]{3,2,1,0:T(8,128)S(1)} %get-tuple-element.6), channel_id=1, source_target_pairs={{1,0},{2,1},{3,2},{4,3},{5,4},{6,5},{7,6},{8,7},{9,8},{10,9},{11,1... | collective-permute-start | bytes 456200 | tf_op jit(solution)/shard_map/ppermute | solution.py:24
  39.7 0.7 broadcast_and_fusion
  40.4 3.3 %copy.59 = f32[32,32,128,4]{2,1,0,3:T(8,128)} copy(f32[32,32,128,4]{2,3,1,0:T(4,128)} %fusion) | data formatting | bytes 4194304 | tf_op jit(solution)/shard_map/cm,mzxy->czxy/dot_general | solution.py:63
  43.7 1.2 dynamic_slice.6
  44.9 1.3 dynamic-slice
  46.8 0.0 collective-permute-done.4
  46.8 0.0 collective-permute-done.5
  46.8 14.4 %fusion.8 = f32[4,34,36,132]{3,2,1,0:T(8,128)S(1)} fusion(f32[4,2,36,132]{3,2,1,0:T(8,128)} %collective-permute-done.5, f32[4,2,36,132]{3,2,1,0:T(8,128)} %collective-permute-done.4, f32[4,32,36,2]{3,2,1,0:T(8,128)} %copy.46, f32[4,32,36,2]{3,2,1,0:T(8,128)S(1)} %copy.45, f32[4,32,2,128]{3,2,1,0:T(2,128)S(1)} %collective-permute-done.1, ...), kind=kLoop, calls=%fused_computation.14 | loop fusion | flops 12925440 | bytes 5322240 | tf_op jit(solution)/shard_map/mul | solution.py:36
  61.2 1.5 %fusion.3 = f32[4,34,34,132]{3,2,1,0:T(8,128)S(1)} fusion(f32[4,34,36,132]{3,2,1,0:T(8,128)S(1)} %fusion.8), kind=kLoop, calls=%fused_computation.7 | loop fusion | flops 2441472 | bytes 9765888 | tf_op jit(solution)/shard_map/mul | solution.py:36
  62.7 3.0 %fusion.1 = f32[4,34,34,130]{3,2,1,0:T(8,128)S(1)} fusion(f32[4,34,34,132]{3,2,1,0:T(8,128)S(1)} %fusion.3), kind=kLoop, calls=%fused_computation.3 | loop fusion | flops 2404480 | bytes 9617920 | tf_op jit(solution)/shard_map/mul | solution.py:36
  65.8 0.0 copy-start.1
  65.8 0.2 fusion.16
  66.0 0.1 fusion.17
  66.1 0.2 fusion.18
  66.3 0.2 fusion.27
  66.6 0.8 copy-done.1
  67.4 1.1 fusion.26
  68.5 0.5 fusion.34
  68.9 0.0 copy-start.2
  68.9 0.3 fusion.21
  69.2 0.2 fusion.19
  69.4 0.1 fusion.28
  69.5 26.1 %all-gather = f32[512,128]{1,0:T(8,128)S(1)} all-gather(f32[32,128]{1,0:T(8,128)S(1)} %fusion.34), channel_id=2, replica_groups=mesh['gx'=8,'gy'=4,'gz'=16] {'gz'}, dimensions={0}, use_global_device_ids=true | all-gather | bytes 278528 | tf_op jit(solution)/shard_map/all_gather | solution.py:94
  95.7 1.0 fusion.50
  96.7 0.7 multiply_add_fusion
  97.4 0.8 multiply_reduce_fusion
  98.3 46.0 %all-reduce = f32[3,32,128]{2,1,0:T(8,128)S(1)} all-reduce(f32[3,32,128]{2,1,0:T(8,128)S(1)} %copy.48), channel_id=3, replica_groups=mesh['gx'=8,'gy'=4,'gz'=16] {'gz'}, use_global_device_ids=true, to_apply=%region_3.4.clone | all-reduce | flops 12288 | bytes 98304
  144.4 0.6 pad_maximum_fusion.12
  (9 shorter events, 0.1 us)
Async XLA Ops:
  0.0 8.0 %copy-start = (f32[4,16]{1,0:T(4,128)S(1)}, f32[4,16]{1,0:T(4,128)}, u32[]{:S(2)}) copy-start(f32[4,16]{1,0:T(4,128)} %param.7) | copy-start | bytes 772
  1.3 11.1 %collective-permute-start = (f32[4,32,2,128]{3,2,1,0:T(2,128)S(1)}, f32[4,32,2,128]{3,2,1,0:T(2,128)S(1)}, u32[]{:S(2)}, u32[]{:S(2)}) collective-permute-start(f32[4,32,2,128]{3,2,1,0:T(2,128)S(1)} %get-tuple-element.9), channel_id=1, source_target_pairs={{0,64},{64,128},{128,192},{192,256},{256,320},{320,384},{384,448},... | collective-permute-start | bytes 393224 | tf_op jit(solution)/shard_map/ppermute | solution.py:22
  6.0 8.1 %collective-permute-start.1 = (f32[4,32,2,128]{3,2,1,0:T(2,128)S(1)}, f32[4,32,2,128]{3,2,1,0:T(2,128)S(1)}, u32[]{:S(2)}, u32[]{:S(2)}) collective-permute-start(f32[4,32,2,128]{3,2,1,0:T(2,128)S(1)} %get-tuple-element.10), channel_id=1, source_target_pairs={{64,0},{128,64},{192,128},{256,192},{320,256},{384,320},{448,384},... | collective-permute-start | bytes 393224 | tf_op jit(solution)/shard_map/ppermute | solution.py:24
  21.1 7.4 %collective-permute-start.2 = (f32[4,32,36,2]{2,1,3,0:T(8,128)S(1)}, f32[4,32,36,2]{2,1,3,0:T(8,128)S(1)}, u32[]{:S(2)}, u32[]{:S(2)}) collective-permute-start(f32[4,32,36,2]{2,1,3,0:T(8,128)S(1)} %copy.43), channel_id=1, source_target_pairs={{0,16},{16,32},{32,48},{1,17},{17,33},{33,49},{2,18},{18,34},{34,5... | collective-permute-start | bytes 110600 | tf_op jit(solution)/shard_map/ppermute | solution.py:22
  25.3 6.9 %collective-permute-start.3 = (f32[4,32,36,2]{2,1,3,0:T(8,128)S(1)}, f32[4,32,36,2]{2,1,3,0:T(8,128)S(1)}, u32[]{:S(2)}, u32[]{:S(2)}) collective-permute-start(f32[4,32,36,2]{2,1,3,0:T(8,128)S(1)} %copy.44), channel_id=1, source_target_pairs={{16,0},{32,16},{48,32},{17,1},{33,17},{49,33},{18,2},{34,18},{50,3... | collective-permute-start | bytes 110600 | tf_op jit(solution)/shard_map/ppermute | solution.py:24
  36.2 10.6 %collective-permute-start.4 = (f32[4,2,36,132]{3,2,1,0:T(8,128)S(1)}, f32[4,2,36,132]{3,2,1,0:T(8,128)}, u32[]{:S(2)}, u32[]{:S(2)}) collective-permute-start(f32[4,2,36,132]{3,2,1,0:T(8,128)S(1)} %get-tuple-element.5), channel_id=1, source_target_pairs={{0,1},{1,2},{2,3},{3,4},{4,5},{5,6},{6,7},{7,8},{8,9},{9,10},{10,1... | collective-permute-start | bytes 456200 | tf_op jit(solution)/shard_map/ppermute | solution.py:22
  38.2 8.6 %collective-permute-start.5 = (f32[4,2,36,132]{3,2,1,0:T(8,128)S(1)}, f32[4,2,36,132]{3,2,1,0:T(8,128)}, u32[]{:S(2)}, u32[]{:S(2)}) collective-permute-start(f32[4,2,36,132]{3,2,1,0:T(8,128)S(1)} %get-tuple-element.6), channel_id=1, source_target_pairs={{1,0},{2,1},{3,2},{4,3},{5,4},{6,5},{7,6},{8,7},{9,8},{10,9},{11,1... | collective-permute-start | bytes 456200 | tf_op jit(solution)/shard_map/ppermute | solution.py:24
  65.8 1.6 %copy-start.1 = (f32[32,32,128,4]{2,1,0,3:T(8,128)S(1)}, f32[32,32,128,4]{2,1,0,3:T(8,128)}, u32[]{:S(2)}) copy-start(f32[32,32,128,4]{2,1,0,3:T(8,128)} %copy.59) | copy-start | bytes 6291460
  68.9 26.7 %copy-start.2 = (s32[16]{0:T(128)S(1)}, s32[16]{0:T(128)}, u32[]{:S(2)}) copy-start(s32[16]{0:T(128)} %param.6) | copy-start | bytes 196
where the time goes:
time: 146 us; the launch traced here: 145 us
  blocking collectives  72.1 us (49%)
  other arithmetic  28.8 us (20%)
  local copies, waits for them, and re-layouts  17.6 us (12%)
  starting transfers between devices  15.9 us (11%)
  matrix products  5.49 us (4%)
  waiting for transfers between devices  4.22 us (3%)
    unnamed x1, blocking collectives  46 us
    all_gather x1, blocking collectives, on_device(): depths = lax.all_gather(depth[None], 'gz', axis=0, tiled=True)  26.1 us
    mul x6, other arithmetic, blur_axis(): return (lower + 2.0 * middle + upper) * 0.25  19.5 us
    ppermute x3, starting transfers between devices, extended(): lax.ppermute(tail, axis, [(i, (i + 1) % count) for i in range(ends)])  9.83 us
    slice x3, local copies, waits for them, and re-layouts, extended(): lax.slice_in_dim(cells, cells.shape[dim] - width, cells.shape[dim], axis=...  6.39 us
    ppermute x3, starting transfers between devices, extended(): lax.ppermute(head, axis, [((i + 1) % count, i) for i in range(ends)])  6.12 us
    dot_general x1, matrix products, shade_brick(): jnp.einsum('cm,mzxy->czxy', table, onehot, precision=lax.Precision.HIGHEST)  4.49 us
    ppermute x3, waiting for transfers between devices, extended(): lax.ppermute(head, axis, [((i + 1) % count, i) for i in range(ends)])  4.21 us
  transfers between devices with their start and end apart: 6, of which 2 were waited for; matrix products, arithmetic and copies ran while one was open for 9% of the time, Pallas kernels for 0%

commit v1 on v0

v1 whole, which is shorter than its diff:
```python
import math

import jax
import jax.numpy as jnp
from jax import lax
from jax.experimental import pallas as pl
from jax.experimental.pallas import tpu as pltpu
from jax.sharding import PartitionSpec as P

MESH = pl.DeviceIdType.MESH
f32 = jnp.float32

BZ = 32
BX = 32
ROW0 = 8
ROWS = 48

OFFSETS = [
    (dz, dx, dy)
    for dz in (-1, 0, 1)
    for dx in (-1, 0, 1)
    for dy in (-1, 0, 1)
    if (dz, dx, dy) != (0, 0, 0)
]


def z_range(dz, width):
    if dz == 1:
        return pl.ds(BZ - width, width), pl.ds(2 - width, width)
    if dz == -1:
        return pl.ds(0, width), pl.ds(2 + BZ, width)
    return pl.ds(0, BZ), pl.ds(2, BZ)


def x_range(dx, width):
    if dx == 1:
        return pl.ds(BX - width, width), pl.ds(ROW0 - width, width)
    if dx == -1:
        return pl.ds(0, width), pl.ds(ROW0 + BX, width)
    return pl.ds(0, BX), pl.ds(ROW0, BX)


def blur3(cells):
    pairs = [a + b for a, b in zip(cells[:-1], cells[1:])]
    return [a + b for a, b in zip(pairs[:-1], pairs[1:])]


def kernel(
    fields, material, order_hbm, table_hbm, out,
    V, M, S, R, WD, WDE, WF, G, D, SM, LK, TB, table, order, SB, RB,
    load_sem, send_sem, recv_sem, a2a_send, a2a_recv,
):
    gz, gx, gy = lax.axis_index("gz"), lax.axis_index("gx"), lax.axis_index("gy")
    nz, nx, ny = lax.axis_size("gz"), lax.axis_size("gx"), lax.axis_size("gy")

    def there(dz, dx, dy):
        ok = None
        for pos, d, n in ((gz, dz, nz), (gx, dx, nx), (gy, dy, ny)):
            if d == 0:
                continue
            this = pos < n - 1 if d == 1 else pos > 0
            ok = this if ok is None else jnp.logical_and(ok, this)
        return ok

    loads = [
        pltpu.make_async_copy(
            fields.at[f], V.at[f, pl.ds(2, BZ), pl.ds(ROW0, BX)], load_sem.at[f]
        )
        for f in range(4)
    ]
    load_m = pltpu.make_async_copy(material, M, load_sem.at[4])
    load_t = pltpu.make_async_copy(table_hbm, table, load_sem.at[5])
    load_o = pltpu.make_async_copy(order_hbm, order, load_sem.at[6])
    for c in loads:
        c.start()
    load_m.start()
    load_t.start()
    load_o.start()

    barrier = pltpu.get_barrier_semaphore()
    for k in range(2, nz):
        for peer, ok in ((gz + k, gz + k < nz), (gz - k, gz - k >= 0)):
            @pl.when(ok)
            def _():
                pl.semaphore_signal(
                    barrier, inc=1, device_id={"gz": peer}, device_id_type=MESH
                )
    for dz, dx, dy in OFFSETS:
        @pl.when(there(dz, dx, dy))
        def _():
            pl.semaphore_signal(
                barrier,
                inc=1,
                device_id={"gz": gz + dz, "gx": gx + dx, "gy": gy + dy},
                device_id_type=MESH,
            )

    def span(pos, n):
        return 1 + (pos > 0).astype(jnp.int32) + (pos < n - 1).astype(jnp.int32)

    expected = span(gz, nz) * span(gx, nx) * span(gy, ny) - span(gz, nz) + nz - 1

    lane = lax.broadcasted_iota(jnp.int32, (8, 128), 1)
    sub = lax.broadcasted_iota(jnp.int32, (8, 128), 0)
    lane4 = lane % 4
    lane_z = lane // 4

    acc = [[jnp.zeros((8, 128), f32)] * 4 for _ in range(4)]
    shift0 = (2, 3, 3, 1)
    for f in range(4):
        loads[f].wait()
        for z in range(BZ):
            mask = lane_z == z
            for i in range(4):
                tile = V[f, z + 2, ROW0 + 8 * i : ROW0 + 8 * i + 8, :]
                moved = pltpu.roll(tile, (4 * z + shift0[f]) % 128, 1)
                acc[f][i] = jnp.where(mask, moved, acc[f][i])
    for i in range(4):
        ad, a1, a2, b = (acc[f][i] for f in range(4))
        front = jnp.where(lane4 < 2, ad, jnp.where(lane4 == 2, a1, pltpu.roll(a2, 1, 1)))
        back = jnp.where(
            lane4 >= 2, ad, jnp.where(lane4 == 0, pltpu.roll(a1, 125, 1), pltpu.roll(a2, 126, 1))
        )
        for s, a in ((0, front), (1, back)):
            rows = pl.ds(8 * i, 8)
            S[s, 0, rows, :] = a
            S[s, 1, rows, :] = b
            S[s, 2, rows, :] = jnp.where(
                lane < 4,
                pltpu.roll(a, 4, 1),
                jnp.where(lane < 8, pltpu.roll(a, 12, 1), pltpu.roll(b, 12, 1)),
            )
            S[s, 3, rows, :] = jnp.where(
                lane >= 124,
                pltpu.roll(a, 124, 1),
                jnp.where(lane >= 120, pltpu.roll(a, 116, 1), pltpu.roll(b, 116, 1)),
            )

    def copies(n, dz, dx, dy):
        device = {"gz": gz + dz, "gx": gx + dx, "gy": gy + dy}

        def make(src, dst, k):
            return pltpu.make_async_remote_copy(
                src_ref=src,
                dst_ref=dst,
                send_sem=send_sem.at[n, k],
                recv_sem=recv_sem.at[n, k],
                device_id=device,
                device_id_type=MESH,
            )

        xs2, xd2 = x_range(dx, 2)
        if dy == 0:
            zs2, zd2 = z_range(dz, 2)
            zs1, zd1 = z_range(dz, 1)
            xs1, xd1 = x_range(dx, 1)
            return [
                make(fields.at[0, zs2, xs2], V.at[0, zd2, xd2], 0),
                make(fields.at[pl.ds(1, 3), zs1, xs1], V.at[pl.ds(1, 3), zd1, xd1], 1),
            ]
        side = 0 if dy == 1 else 1
        kinds = {0: pl.ds(0, 2), 1: pl.ds(2, 1), -1: pl.ds(3, 1)}[dz]
        return [make(S.at[side, kinds, xs2], R.at[side, kinds, xd2], 0)]

    pl.semaphore_wait(barrier, expected)
    for n, (dz, dx, dy) in enumerate(OFFSETS):
        @pl.when(there(dz, dx, dy))
        def _():
            for c in copies(n, dz, dx, dy):
                c.start()

    zrow = jnp.zeros((2, 128), f32)

    @pl.when(gx == 0)
    def _():
        for s in range(2):
            for k in range(4):
                R[s, k, ROW0 - 2 : ROW0, :] = zrow

        @pl.loop(0, BZ + 4)
        def _(z):
            for f in range(4):
                V[f, z, ROW0 - 2 : ROW0, :] = zrow

    @pl.when(gx == nx - 1)
    def _():
        for s in range(2):
            for k in range(4):
                R[s, k, ROW0 + BX : ROW0 + BX + 2, :] = zrow

        @pl.loop(0, BZ + 4)
        def _(z):
            for f in range(4):
                V[f, z, ROW0 + BX : ROW0 + BX + 2, :] = zrow

    zrows = jnp.zeros((BX + 4, 128), f32)

    def clear_planes(planes, kind):
        for s in range(2):
            R[s, kind, ROW0 - 2 : ROW0 + BX + 2, :] = zrows
        for f in range(4):
            for z in planes:
                V[f, z, ROW0 - 2 : ROW0 + BX + 2, :] = zrows

    @pl.when(gz == 0)
    def _():
        clear_planes((0, 1), 2)

    @pl.when(gz == nz - 1)
    def _():
        clear_planes((BZ + 2, BZ + 3), 3)

    for s, edge in ((0, 0), (1, ny - 1)):
        @pl.when(gy == edge)
        def _():
            for k in range(4):
                R[s, k, ROW0 - 2 : ROW0 + BX + 2, :] = zrows

    load_m.wait()
    load_t.wait()
    load_o.wait()
    depth_total = BZ * nz
    TB[...] = jnp.zeros(TB.shape, f32)
    for c in range(4):
        entries = jnp.broadcast_to(table[c : c + 1, :], (8, table.shape[1]))
        TB[c, :, 0 : table.shape[1]] = entries * (2.0 / depth_total) if c == 3 else entries

    @pl.loop(0, BZ)
    def _(z):
        tables = [TB[c] for c in range(4)]
        for j in range(4):
            index = M[z, pl.ds(j, 8, stride=4), :]
            for c in range(4):
                LK[z, c, j] = jnp.take_along_axis(tables[c], index, axis=1)

    for n, (dz, dx, dy) in enumerate(OFFSETS):
        @pl.when(there(-dz, -dx, -dy))
        def _():
            for c in copies(n, dz, dx, dy):
                c.wait_recv()

    on = lambda cond: cond.astype(f32)
    low_x = jnp.where(sub == 0, on(gx > 0), 1.0)
    high_x = jnp.where(sub == 7, on(gx < nx - 1), 1.0)
    low_z, high_z = on(gz > 0), on(gz < nz - 1)
    y_first = jnp.where(lane == 0, on(gy == 0), 0.0)
    y_last = jnp.where(lane == 127, on(gy == ny - 1), 0.0)
    six = 6.0 - y_first - y_last
    edge_sign = y_first - y_last

    def x_mask(cells):
        return [cells[0] * low_x] + cells[1:5] + [cells[5] * high_x]

    def packed(s, k, js):
        return [R[s, k, pl.ds(ROW0 + j, 8, stride=4), :] for j in js]

    js = range(-2, 6)
    near = [packed(0, k, js) for k in range(4)]
    far = [packed(1, k, js) for k in range(4)]
    dens = [
        blur3([jnp.where(lane4 < 2, a, b) for a, b in zip(near[k], far[k])]) for k in (0, 2, 3)
    ]
    for j in range(6):
        u, lo, hi = dens[0][j], dens[1][j], dens[2][j]
        below = jnp.where(lane < 4, lo, pltpu.roll(u, 4, 1))
        above = jnp.where(lane >= 124, hi, pltpu.roll(u, 124, 1))
        mask = low_x if j == 0 else high_x if j == 5 else None
        w = below + 2.0 * u + above
        w_lo = (pltpu.roll(lo, 124, 1) + 2.0 * lo + u) * low_z
        w_hi = (pltpu.roll(hi, 4, 1) + 2.0 * hi + u) * high_z
        if mask is not None:
            w, w_lo, w_hi = w * mask, w_lo * mask, w_hi * mask
        WD[j] = w
        WDE[0, j] = w_lo
        WDE[1, j] = w_hi

    def pair(f, k):
        cells = []
        for a, b in zip(near[k][1:7], far[k][1:7]):
            if f == 1:
                cells.append(jnp.where(lane4 == 2, a, pltpu.roll(b, 3, 1)))
            elif f == 2:
                cells.append(jnp.where(lane4 == 2, pltpu.roll(a, 127, 1), pltpu.roll(b, 2, 1)))
            else:
                cells.append(jnp.where(lane4 == 0, a, b))
        return blur3(cells)

    for f in (1, 2, 3):
        main = pair(f, 1 if f == 3 else 0)
        lo, hi = pair(f, 2), pair(f, 3)
        for j in range(4):
            lo_j, hi_j = lo[j], hi[j]
            if f == 3:
                lo_j, hi_j = pltpu.roll(lo_j, 120, 1), pltpu.roll(hi_j, 8, 1)
            below = jnp.where(lane < 4, lo_j, pltpu.roll(main[j], 4, 1))
            above = jnp.where(lane >= 124, hi_j, pltpu.roll(main[j], 124, 1))
            WF[f - 1, j] = below + 2.0 * main[j] + above

    first, last = lane == 0, lane == 127
    first2, last2 = lane <= 1, lane >= 126

    def x_blur(f, plane, js):
        return blur3([V[f, plane, pl.ds(ROW0 + j, 8, stride=4), :] for j in js])

    def density_plane(z, w, edges):
        by, sy = [], []
        for j in range(6):
            a, e = w[j], edges[j]
            l1 = pltpu.roll(jnp.where(last, e, a), 1, 1)
            l2 = pltpu.roll(jnp.where(last2, e, a), 2, 1)
            r1 = pltpu.roll(jnp.where(first, e, a), 127, 1)
            r2 = pltpu.roll(jnp.where(first2, e, a), 126, 1)
            p1, m1 = l1 + r1, r1 - l1
            by.append((l2 + r2) + 4.0 * p1 + a * six)
            sy.append((r2 - l2) + 2.0 * m1 + a * edge_sign)
            if 1 <= j <= 4:
                D[z + 1, j - 1] = p1 + 2.0 * a
        bb = blur3(by)
        bs = blur3(sy)
        for j in range(4):
            G[0, z + 1, j] = bb[j]
            G[1, z + 1, j] = by[j + 2] - by[j]
            G[2, z + 1, j] = bs[j]

    def blend(a, b, c):
        return [p + 2.0 * q + r for p, q, r in zip(a, b, c)]

    u0 = x_blur(0, 0, js)
    u1 = x_blur(0, 1, js)
    u2 = x_blur(0, 2, js)
    w = x_mask([x * low_z for x in blend(u0, u1, u2)])
    density_plane(-1, w, [pltpu.roll(WDE[0, j], 126, 1) for j in range(6)])

    def density_step(z, carry):
        before, here = carry[:6], carry[6:]
        after = x_blur(0, z + 3, js)
        w = x_mask(blend(before, here, after))
        amount = lax.rem(126 - 4 * z + 128, 128)
        density_plane(z, w, [pltpu.roll(WD[j], amount, 1) for j in range(6)])
        return tuple(here) + tuple(after)

    def density_two(i, carry):
        return density_step(2 * i + 1, density_step(2 * i, carry))

    carry = lax.fori_loop(0, BZ // 2, density_two, tuple(u1) + tuple(u2))
    u3 = x_blur(0, BZ + 3, js)
    w = x_mask([x * high_z for x in blend(carry[:6], carry[6:], u3)])
    density_plane(BZ, w, [pltpu.roll(WDE[1, j], 2, 1) for j in range(6)])

    js1 = range(-1, 5)

    def field_step(z, carry):
        new = []
        for f in (1, 2, 3):
            before = carry[8 * (f - 1) : 8 * (f - 1) + 4]
            here = carry[8 * (f - 1) + 4 : 8 * f]
            after = x_blur(f, z + 3, js1)
            w = blend(before, here, after)
            amount = lax.rem((127 if f == 3 else 125) - 4 * z + 128, 128)
            for j in range(4):
                e = pltpu.roll(WF[f - 1, j], amount, 1)
                l1 = pltpu.roll(jnp.where(last, e, w[j]), 1, 1)
                r1 = pltpu.roll(jnp.where(first, e, w[j]), 127, 1)
                SM[z, f - 1, j] = l1 + r1 + 2.0 * w[j]
            new += list(here) + list(after)
        return tuple(new)

    def field_two(i, carry):
        return field_step(2 * i + 1, field_step(2 * i, carry))

    carry = []
    for f in (1, 2, 3):
        carry += x_blur(f, 1, js1) + x_blur(f, 2, js1)
    lax.fori_loop(0, BZ // 2, field_two, tuple(carry))

    to_exp2 = 3.0 / (64.0 * math.log(2.0))

    def shade_step(z, carry):
        light, depth, red, green, blue = (list(carry[4 * k : 4 * k + 4]) for k in range(5))
        colour = [red, green, blue]
        for j in range(4):
            g_z = G[0, z + 2, j] - G[0, z, j]
            g_x = G[1, z, j] + 2.0 * G[1, z + 1, j] + G[1, z + 2, j]
            g_y = G[2, z, j] + 2.0 * G[2, z + 1, j] + G[2, z + 2, j]
            facing = jnp.abs(2.0 * (g_z + g_y) + g_x)
            norm = g_z * g_z + g_x * g_x + g_y * g_y + 0.0025 * 2048.0 * 2048.0
            shading = 0.3 + 0.4 * facing * lax.rsqrt(norm)
            grown = jnp.exp2(D[z + 1, j] * to_exp2)
            soft = jnp.where(
                grown < 1.0 / 128.0,
                grown * (1.0 + grown * (-0.5 + grown * (1.0 / 3.0))),
                jnp.log(1.0 + grown),
            )
            e = LK[z, 3, j] * soft
            taken = e * (
                1.0 + e * (-0.5 + e * (1.0 / 6.0 + e * (-1.0 / 24.0 + e * (1.0 / 120.0))))
            )
            weight = light[j] * taken
            light[j] = light[j] - weight
            depth[j] = depth[j] + e
            lit = weight * shading
            for c in range(3):
                tone = 1.0 + 0.5 * jnp.tanh(SM[z, c, j] * (1.0 / 64.0))
                colour[c][j] = colour[c][j] + lit * (LK[z, c, j] * tone)
        return tuple(light + depth + colour[0] + colour[1] + colour[2])

    def shade_two(i, carry):
        return shade_step(2 * i + 1, shade_step(2 * i, carry))

    zero = jnp.zeros((8, 128), f32)
    final = lax.fori_loop(
        0, BZ // 2, shade_two, tuple([jnp.ones((8, 128), f32)] * 4 + [zero] * 16)
    )

    for c, k in ((0, 2), (1, 3), (2, 4), (3, 1)):
        for j in range(4):
            SB[pl.ds(8 * (j // 2) + 2 * c + j % 2, 8, stride=16), :] = final[4 * k + j]

    def to_peer(k):
        peer = lax.rem(gz + k, nz)
        return pltpu.make_async_remote_copy(
            src_ref=SB.at[pl.ds(pl.multiple_of(peer * 8, 8), 8)],
            dst_ref=RB.at[pl.ds(pl.multiple_of(gz * 8, 8), 8)],
            send_sem=a2a_send.at[k],
            recv_sem=a2a_recv.at[k],
            device_id={"gz": peer},
            device_id_type=MESH,
        )

    far_first = sorted(range(1, nz), key=lambda k: (-min(k, nz - k), k))
    for k in far_first:
        to_peer(k).start()
    own = pl.ds(pl.multiple_of(gz * 8, 8), 8)
    RB[own, :] = SB[own, :]
    for n, (dz, dx, dy) in enumerate(OFFSETS):
        @pl.when(there(dz, dx, dy))
        def _():
            for c in copies(n, dz, dx, dy):
                c.wait_send()
    for k in reversed(far_first):
        to_peer(k).wait_recv()

    parts = [RB[8 * b : 8 * b + 8, :] for b in range(nz)]
    depths = []
    for part in parts:
        d = jnp.where(sub >= 6, part, 0.0)
        d = d + pltpu.roll(d, 4, 0)
        depths.append(d + pltpu.roll(d, 2, 0))
    total = depths[0]
    for d in depths[1:]:
        total = total + d
    image = zero
    for b in range(nz):
        prior = zero
        for o in range(nz):
            if o != b:
                prior = prior + jnp.where(order[o] < order[b], depths[o], 0.0)
        image = image + jnp.exp(-prior) * parts[b]
    small = total * (
        1.0 + total * (-0.5 + total * (1.0 / 6.0 + total * (-1.0 / 24.0 + total * (1.0 / 120.0))))
    )
    opacity = jnp.where(total < 0.125, small, 1.0 - jnp.exp(-total))
    image = jnp.where(sub >= 6, opacity, image)
    for c in range(4):
        out[c] = image[2 * c : 2 * c + 2, :]
    for k in far_first:
        to_peer(k).wait_send()


def on_device(fields, material, depth_order, table):
    vmem = lambda *shape: pltpu.VMEM(shape, f32)
    dma = pltpu.SemaphoreType.DMA
    count = len(OFFSETS)
    return pl.pallas_call(
        kernel,
        out_shape=jax.ShapeDtypeStruct((4, 2, 128), f32),
        in_specs=[pl.BlockSpec(memory_space=pl.ANY)] * 4,
        out_specs=pl.BlockSpec(memory_space=pltpu.VMEM),
        scratch_shapes=[
            vmem(4, BZ + 4, ROWS, 128),
            pltpu.VMEM((BZ, BX, 128), jnp.int32),
            vmem(2, 4, BX, 128),
            vmem(2, 4, ROWS, 128),
            vmem(6, 8, 128),
            vmem(2, 6, 8, 128),
            vmem(3, 4, 8, 128),
            vmem(3, BZ + 2, 4, 8, 128),
            vmem(BZ + 2, 4, 8, 128),
            vmem(BZ, 3, 4, 8, 128),
            vmem(BZ, 4, 4, 8, 128),
            vmem(4, 8, 128),
            vmem(4, 16),
            pltpu.SMEM((16,), jnp.int32),
            vmem(128, 128),
            vmem(128, 128),
            dma((7,)),
            dma((count, 2)),
            dma((count, 2)),
            dma((16,)),
            dma((16,)),
        ],
        compiler_params=pltpu.CompilerParams(collective_id=0, has_side_effects=True),
    )(fields, material, depth_order, table)


def solution(mesh):
    return jax.shard_map(
        on_device,
        mesh=mesh,
        in_specs=(P(None, "gz", "gx", "gy"), P("gz", "gx", "gy"), P(), P()),
        out_specs=P(None, ("gx", "gz"), "gy"),
        check_vma=False,
    )
```

time: 146 us -> 35.2 us (0.24)
  the two profiles are of different devices: /device:TPU:28 before, /device:TPU:25 now
where the time goes in v1:
time: 35.2 us; the launch traced here: 35 us
  Pallas kernels  33.7 us (96%)
  local copies, waits for them, and re-layouts  1.28 us (4%)
    pallas_call x1, Pallas kernels, on_device(): pl.pallas_call(kernel, out_shape=jax.ShapeDtypeStruct((4, 2, 128), f32),...  33.7 us
    unnamed x1, local copies, waits for them, and re-layouts  1.28 us

profile of v1, /device:TPU:25, one launch (start us, length us, event | category | flops | bytes accessed | tf_op | source)
XLA Modules:
  0.0 35.0 jit_solution(16193631169261178256)
XLA Ops:
  0.0 33.7 %shard_map.46 = f32[4,2,128]{2,1,0:T(2,128)} custom-call(f32[4,32,32,128]{3,2,1,0:T(8,128)} %fields.1, s32[32,32,128]{2,1,0:T(8,128)} %material.1, s32[16]{0:T(128)} %order_hbm.1, f32[4,16]{1,0:T(4,128)} %table_hbm.1), custom_call_target="tpu_custom_call" | custom-call | tf_op jit(solution)/shard_map/pallas_call | solution.py:474
  33.7 1.3 %copy.6 = f32[4,2,128]{2,1,0:T(2,128)} copy(f32[4,2,128]{2,1,0:T(2,128)} %shard_map.46) | data formatting | bytes 8192

commit v2 on v1

--- a/solution.py
+++ b/solution.py
@@ -22,6 +22,7 @@
     for dy in (-1, 0, 1)
     if (dz, dx, dy) != (0, 0, 0)
 ]
+OFFSETS.sort(key=lambda o: -abs(o[0]) - abs(o[1]) - abs(o[2]))
 
 
 def z_range(dz, width):
@@ -48,7 +49,7 @@
 def kernel(
     fields, material, order_hbm, table_hbm, out,
     V, M, S, R, WD, WDE, WF, G, D, SM, LK, TB, table, order, SB, RB,
-    load_sem, send_sem, recv_sem, a2a_send, a2a_recv,
+    load_sem, send_sem, recv_sem, a2a_send, a2a_recv, greeted,
 ):
     gz, gx, gy = lax.axis_index("gz"), lax.axis_index("gx"), lax.axis_index("gy")
     nz, nx, ny = lax.axis_size("gz"), lax.axis_size("gx"), lax.axis_size("gy")
@@ -78,13 +79,6 @@
     load_o.start()
 
     barrier = pltpu.get_barrier_semaphore()
-    for k in range(2, nz):
-        for peer, ok in ((gz + k, gz + k < nz), (gz - k, gz - k >= 0)):
-            @pl.when(ok)
-            def _():
-                pl.semaphore_signal(
-                    barrier, inc=1, device_id={"gz": peer}, device_id_type=MESH
-                )
     for dz, dx, dy in OFFSETS:
         @pl.when(there(dz, dx, dy))
         def _():
@@ -95,10 +89,24 @@
                 device_id_type=MESH,
             )
 
+    at_end = jnp.logical_or(gz == 0, gz == nz - 1)
+
+    @pl.when(at_end)
+    def _():
+        pl.semaphore_signal(
+            barrier, inc=1, device_id={"gz": nz - 1 - gz}, device_id_type=MESH
+        )
+
+    def greet(k):
+        for step in (1 << k, nz - (1 << k)):
+            pl.semaphore_signal(
+                greeted.at[k], inc=1, device_id={"gz": lax.rem(gz + step, nz)}, device_id_type=MESH
+            )
+
     def span(pos, n):
         return 1 + (pos > 0).astype(jnp.int32) + (pos < n - 1).astype(jnp.int32)
 
-    expected = span(gz, nz) * span(gx, nx) * span(gy, ny) - span(gz, nz) + nz - 1
+    expected = span(gz, nz) * span(gx, nx) * span(gy, ny) - 1 + at_end.astype(jnp.int32)
 
     lane = lax.broadcasted_iota(jnp.int32, (8, 128), 1)
     sub = lax.broadcasted_iota(jnp.int32, (8, 128), 0)
@@ -169,6 +177,8 @@
             for c in copies(n, dz, dx, dy):
                 c.start()
 
+    greet(0)
+
     zrow = jnp.zeros((2, 128), f32)
 
     @pl.when(gx == 0)
@@ -238,6 +248,9 @@
         def _():
             for c in copies(n, dz, dx, dy):
                 c.wait_recv()
+
+    pl.semaphore_wait(greeted.at[0], 2)
+    greet(1)
 
     on = lambda cond: cond.astype(f32)
     low_x = jnp.where(sub == 0, on(gx > 0), 1.0)
@@ -347,6 +360,9 @@
     w = x_mask([x * high_z for x in blend(carry[:6], carry[6:], u3)])
     density_plane(BZ, w, [pltpu.roll(WDE[1, j], 2, 1) for j in range(6)])
 
+    pl.semaphore_wait(greeted.at[1], 2)
+    greet(2)
+
     js1 = range(-1, 5)
 
     def field_step(z, carry):
@@ -411,6 +427,8 @@
     final = lax.fori_loop(
         0, BZ // 2, shade_two, tuple([jnp.ones((8, 128), f32)] * 4 + [zero] * 16)
     )
+
+    pl.semaphore_wait(greeted.at[2], 2)
 
     for c, k in ((0, 2), (1, 3), (2, 4), (3, 1)):
         for j in range(4):
@@ -473,7 +491,7 @@
     count = len(OFFSETS)
     return pl.pallas_call(
         kernel,
-        out_shape=jax.ShapeDtypeStruct((4, 2, 128), f32),
+        out_shape=pltpu.VMEM((4, 2, 128), f32),
         in_specs=[pl.BlockSpec(memory_space=pl.ANY)] * 4,
         out_specs=pl.BlockSpec(memory_space=pltpu.VMEM),
         scratch_shapes=[
@@ -498,6 +516,7 @@
             dma((count, 2)),
             dma((16,)),
             dma((16,)),
+            pltpu.SemaphoreType.REGULAR((3,)),
         ],
         compiler_params=pltpu.CompilerParams(collective_id=0, has_side_effects=True),
     )(fields, material, depth_order, table)

time: 35.2 us -> 31.6 us (0.90)
  the two profiles are of different devices: /device:TPU:25 before, /device:TPU:17 now
where the time goes in v2:
time: 31.6 us; the launch traced here: 31.4 us
  Pallas kernels  30.8 us (97%)
  local copies, waits for them, and re-layouts  0.6 us (2%)
    pallas_call x1, Pallas kernels, on_device(): pl.pallas_call(kernel, out_shape=pltpu.VMEM((4, 2, 128), f32), in_specs=[...  30.8 us

profile of v2, /device:TPU:17, one launch (start us, length us, event | category | flops | bytes accessed | tf_op | source)
XLA Modules:
  0.0 31.4 jit_solution(17100502275332667055)
XLA Ops:
  0.0 30.8 %shard_map.46 = f32[4,2,128]{2,1,0:T(2,128)S(1)} custom-call(f32[4,32,32,128]{3,2,1,0:T(8,128)} %fields.1, s32[32,32,128]{2,1,0:T(8,128)} %material.1, s32[16]{0:T(128)} %order_hbm.1, f32[4,16]{1,0:T(4,128)} %table_hbm.1), custom_call_target="tpu_custom_call" | custom-call | tf_op jit(solution)/shard_map/pallas_call | solution.py:492
  30.9 0.6 %copy.6 = f32[4,2,128]{2,1,0:T(2,128)} copy(f32[4,2,128]{2,1,0:T(2,128)S(1)} %shard_map.46) | data formatting | bytes 8192

commit v3 on v1

--- a/solution.py
+++ b/solution.py
@@ -9,6 +9,7 @@
 
 MESH = pl.DeviceIdType.MESH
 f32 = jnp.float32
+bf16 = jnp.bfloat16
 
 BZ = 32
 BX = 32
@@ -22,6 +23,7 @@
     for dy in (-1, 0, 1)
     if (dz, dx, dy) != (0, 0, 0)
 ]
+OFFSETS.sort(key=lambda o: -abs(o[0]) - abs(o[1]) - abs(o[2]))
 
 
 def z_range(dz, width):
@@ -45,10 +47,34 @@
     return [a + b for a, b in zip(pairs[:-1], pairs[1:])]
 
 
+def split(a):
+    high = a.astype(bf16)
+    rest = a - high.astype(f32)
+    middle = rest.astype(bf16)
+    return high, middle, (rest - middle.astype(f32)).astype(bf16)
+
+
+def blur_weight(d):
+    return jnp.where(d == 0, 2.0, jnp.where(jnp.abs(d) == 1, 1.0, 0.0))
+
+
+def blur2_weight(d):
+    far = jnp.abs(d)
+    return jnp.where(
+        far == 0, 6.0, jnp.where(far == 1, 4.0, jnp.where(far == 2, 1.0, 0.0))
+    )
+
+
+def slope_weight(d):
+    far = jnp.abs(d)
+    size = jnp.where(far == 1, 2.0, jnp.where(far == 2, 1.0, 0.0))
+    return jnp.where(d > 0, size, -size)
+
+
 def kernel(
     fields, material, order_hbm, table_hbm, out,
-    V, M, S, R, WD, WDE, WF, G, D, SM, LK, TB, table, order, SB, RB,
-    load_sem, send_sem, recv_sem, a2a_send, a2a_recv,
+    V, M, S, R, PE, H, TD, TF, DD, SM, LK, TB, table, order, at_rank, SB, RB,
+    load_sem, send_sem, recv_sem, a2a_send, a2a_recv, greeted,
 ):
     gz, gx, gy = lax.axis_index("gz"), lax.axis_index("gx"), lax.axis_index("gy")
     nz, nx, ny = lax.axis_size("gz"), lax.axis_size("gx"), lax.axis_size("gy")
@@ -78,13 +104,6 @@
     load_o.start()
 
     barrier = pltpu.get_barrier_semaphore()
-    for k in range(2, nz):
-        for peer, ok in ((gz + k, gz + k < nz), (gz - k, gz - k >= 0)):
-            @pl.when(ok)
-            def _():
-                pl.semaphore_signal(
-                    barrier, inc=1, device_id={"gz": peer}, device_id_type=MESH
-                )
     for dz, dx, dy in OFFSETS:
         @pl.when(there(dz, dx, dy))
         def _():
@@ -95,10 +114,22 @@
                 device_id_type=MESH,
             )
 
+    def greet(k):
+        for to in (gz + (1 << k), gz - (1 << k)):
+            @pl.when(jnp.logical_and(to >= 0, to < nz))
+            def _():
+                pl.semaphore_signal(
+                    greeted.at[k], inc=1, device_id={"gz": to}, device_id_type=MESH
+                )
+
+    def await_greetings(k):
+        count = (gz >= 1 << k).astype(jnp.int32) + (gz + (1 << k) < nz).astype(jnp.int32)
+        pl.semaphore_wait(greeted.at[k], count)
+
     def span(pos, n):
         return 1 + (pos > 0).astype(jnp.int32) + (pos < n - 1).astype(jnp.int32)
 
-    expected = span(gz, nz) * span(gx, nx) * span(gy, ny) - span(gz, nz) + nz - 1
+    expected = span(gz, nz) * span(gx, nx) * span(gy, ny) - 1
 
     lane = lax.broadcasted_iota(jnp.int32, (8, 128), 1)
     sub = lax.broadcasted_iota(jnp.int32, (8, 128), 0)
@@ -169,6 +200,8 @@
             for c in copies(n, dz, dx, dy):
                 c.start()
 
+    greet(0)
+
     zrow = jnp.zeros((2, 128), f32)
 
     @pl.when(gx == 0)
@@ -216,22 +249,62 @@
             for k in range(4):
                 R[s, k, ROW0 - 2 : ROW0 + BX + 2, :] = zrows
 
+    await_greetings(0)
+    greet(1)
+
     load_m.wait()
     load_t.wait()
     load_o.wait()
+    for rank in range(nz):
+        layer = 0
+        for o in range(nz):
+            layer = jnp.where(order[o] == rank, o, layer)
+        at_rank[rank] = layer
     depth_total = BZ * nz
-    TB[...] = jnp.zeros(TB.shape, f32)
     for c in range(4):
-        entries = jnp.broadcast_to(table[c : c + 1, :], (8, table.shape[1]))
-        TB[c, :, 0 : table.shape[1]] = entries * (2.0 / depth_total) if c == 3 else entries
+        for m in range(16):
+            entry = table[c, m] * (2.0 / depth_total) if c == 3 else table[c, m]
+            TB[16 * c + m] = jnp.broadcast_to(entry, (8, 128))
+
+    row = lax.broadcasted_iota(jnp.int32, (128, 128), 0)
+    col = lax.broadcasted_iota(jnp.int32, (128, 128), 1)
+    row4 = row % 4
+    beside = jnp.where(row4 < 2, row4 - 2, row4 + 126)
+    beside1 = jnp.where(row4 == 2, -1, jnp.where(row4 == 3, 128, -1000))
+    first_y = jnp.where((row == 0) & (col == 0), (gy == 0).astype(f32), 0.0)
+    last_y = jnp.where((row == 127) & (col == 127), (gy == ny - 1).astype(f32), 0.0)
+    own = jnp.concatenate(
+        [
+            blur_weight(row - col),
+            blur2_weight(row - col) - first_y - last_y,
+            slope_weight(row - col) + first_y - last_y,
+        ],
+        axis=1,
+    ).astype(bf16)
+    for k in range(3):
+        TD[128 * k : 128 * k + 128, :] = own
+        TF[128 * k : 128 * k + 128, :] = own[:, 0:128]
+    TD[384:512, :] = jnp.concatenate(
+        [weight(beside - col) for weight in (blur_weight, blur2_weight, slope_weight)], axis=1
+    ).astype(bf16)
+    TF[384:512, :] = blur_weight(beside1 - col).astype(bf16)
 
     @pl.loop(0, BZ)
     def _(z):
-        tables = [TB[c] for c in range(4)]
+        bits = []
         for j in range(4):
             index = M[z, pl.ds(j, 8, stride=4), :]
-            for c in range(4):
-                LK[z, c, j] = jnp.take_along_axis(tables[c], index, axis=1)
+            bits.append([(index & (1 << k)) != 0 for k in range(4)])
+        for c in range(4):
+            entries = [TB[16 * c + m] for m in range(16)]
+            for j in range(4):
+                left = entries
+                for k in range(4):
+                    left = [jnp.where(bits[j][k], b, a) for a, b in zip(left[::2], left[1::2])]
+                LK[z, c, j] = left[0]
+
+    await_greetings(1)
+    greet(2)
 
     for n, (dz, dx, dy) in enumerate(OFFSETS):
         @pl.when(there(-dz, -dx, -dy))
@@ -239,15 +312,13 @@
             for c in copies(n, dz, dx, dy):
                 c.wait_recv()
 
+    await_greetings(2)
+    greet(3)
+
     on = lambda cond: cond.astype(f32)
     low_x = jnp.where(sub == 0, on(gx > 0), 1.0)
     high_x = jnp.where(sub == 7, on(gx < nx - 1), 1.0)
     low_z, high_z = on(gz > 0), on(gz < nz - 1)
-    y_first = jnp.where(lane == 0, on(gy == 0), 0.0)
-    y_last = jnp.where(lane == 127, on(gy == ny - 1), 0.0)
-    six = 6.0 - y_first - y_last
-    edge_sign = y_first - y_last
-
     def x_mask(cells):
         return [cells[0] * low_x] + cells[1:5] + [cells[5] * high_x]
 
@@ -260,6 +331,7 @@
     dens = [
         blur3([jnp.where(lane4 < 2, a, b) for a, b in zip(near[k], far[k])]) for k in (0, 2, 3)
     ]
+    packed_main, packed_low, packed_high = [], [], []
     for j in range(6):
         u, lo, hi = dens[0][j], dens[1][j], dens[2][j]
         below = jnp.where(lane < 4, lo, pltpu.roll(u, 4, 1))
@@ -270,9 +342,20 @@
         w_hi = (pltpu.roll(hi, 4, 1) + 2.0 * hi + u) * high_z
         if mask is not None:
             w, w_lo, w_hi = w * mask, w_lo * mask, w_hi * mask
-        WD[j] = w
-        WDE[0, j] = w_lo
-        WDE[1, j] = w_hi
+        packed_main.append(w)
+        packed_low.append(w_lo)
+        packed_high.append(w_hi)
+
+    def keep(slot, cells):
+        for p in range(len(cells) // 2):
+            parts = split(jnp.concatenate([cells[2 * p], cells[2 * p + 1]], axis=0))
+            for k in range(3):
+                part = parts[k].astype(f32)
+                PE[slot, p, k] = pltpu.roll(part, 44 * k, 1) if k else part
+
+    keep(0, packed_main)
+    keep(1, packed_low)
+    keep(2, packed_high)
 
     def pair(f, k):
         cells = []
@@ -282,61 +365,51 @@
             elif f == 2:
                 cells.append(jnp.where(lane4 == 2, pltpu.roll(a, 127, 1), pltpu.roll(b, 2, 1)))
             else:
-                cells.append(jnp.where(lane4 == 0, a, b))
+                cells.append(pltpu.roll(jnp.where(lane4 == 0, a, b), 2, 1))
         return blur3(cells)
 
     for f in (1, 2, 3):
         main = pair(f, 1 if f == 3 else 0)
         lo, hi = pair(f, 2), pair(f, 3)
+        cells = []
         for j in range(4):
             lo_j, hi_j = lo[j], hi[j]
             if f == 3:
                 lo_j, hi_j = pltpu.roll(lo_j, 120, 1), pltpu.roll(hi_j, 8, 1)
             below = jnp.where(lane < 4, lo_j, pltpu.roll(main[j], 4, 1))
             above = jnp.where(lane >= 124, hi_j, pltpu.roll(main[j], 124, 1))
-            WF[f - 1, j] = below + 2.0 * main[j] + above
-
-    first, last = lane == 0, lane == 127
-    first2, last2 = lane <= 1, lane >= 126
+            cells.append(below + 2.0 * main[j] + above)
+        keep(2 + f, cells)
 
     def x_blur(f, plane, js):
         return blur3([V[f, plane, pl.ds(ROW0 + j, 8, stride=4), :] for j in js])
 
-    def density_plane(z, w, edges):
-        by, sy = [], []
-        for j in range(6):
-            a, e = w[j], edges[j]
-            l1 = pltpu.roll(jnp.where(last, e, a), 1, 1)
-            l2 = pltpu.roll(jnp.where(last2, e, a), 2, 1)
-            r1 = pltpu.roll(jnp.where(first, e, a), 127, 1)
-            r2 = pltpu.roll(jnp.where(first2, e, a), 126, 1)
-            p1, m1 = l1 + r1, r1 - l1
-            by.append((l2 + r2) + 4.0 * p1 + a * six)
-            sy.append((r2 - l2) + 2.0 * m1 + a * edge_sign)
-            if 1 <= j <= 4:
-                D[z + 1, j - 1] = p1 + 2.0 * a
-        bb = blur3(by)
-        bs = blur3(sy)
-        for j in range(4):
-            G[0, z + 1, j] = bb[j]
-            G[1, z + 1, j] = by[j + 2] - by[j]
-            G[2, z + 1, j] = bs[j]
-
     def blend(a, b, c):
         return [p + 2.0 * q + r for p, q, r in zip(a, b, c)]
+
+    group = lax.broadcasted_iota(jnp.int32, (16, 128), 1) // 4
+
+    def put(base, slot, cells, z):
+        masks = [group == lax.rem(z + 11 * k, BZ) for k in range(3)]
+        for p in range(len(cells) // 2):
+            rows = pl.ds(pl.multiple_of(base + 16 * p, 16), 16)
+            parts = split(jnp.concatenate([cells[2 * p], cells[2 * p + 1]], axis=0))
+            for k in range(3):
+                H[rows, 128 * k : 128 * k + 128] = parts[k]
+            beside = jnp.where(masks[2], PE[slot, p, 2], 0.0)
+            beside = jnp.where(masks[1], PE[slot, p, 1], beside)
+            beside = jnp.where(masks[0], PE[slot, p, 0], beside)
+            H[rows, 384:512] = beside.astype(bf16)
 
     u0 = x_blur(0, 0, js)
     u1 = x_blur(0, 1, js)
     u2 = x_blur(0, 2, js)
-    w = x_mask([x * low_z for x in blend(u0, u1, u2)])
-    density_plane(-1, w, [pltpu.roll(WDE[0, j], 126, 1) for j in range(6)])
+    put(0, 1, x_mask([x * low_z for x in blend(u0, u1, u2)]), 0)
 
     def density_step(z, carry):
         before, here = carry[:6], carry[6:]
         after = x_blur(0, z + 3, js)
-        w = x_mask(blend(before, here, after))
-        amount = lax.rem(126 - 4 * z + 128, 128)
-        density_plane(z, w, [pltpu.roll(WD[j], amount, 1) for j in range(6)])
+        put(48 * z + 48, 0, x_mask(blend(before, here, after)), z)
         return tuple(here) + tuple(after)
 
     def density_two(i, carry):
@@ -344,8 +417,10 @@
 
     carry = lax.fori_loop(0, BZ // 2, density_two, tuple(u1) + tuple(u2))
     u3 = x_blur(0, BZ + 3, js)
-    w = x_mask([x * high_z for x in blend(carry[:6], carry[6:], u3)])
-    density_plane(BZ, w, [pltpu.roll(WDE[1, j], 2, 1) for j in range(6)])
+    put(48 * BZ + 48, 2, x_mask([x * high_z for x in blend(carry[:6], carry[6:], u3)]), BZ - 1)
+    for k in range(2):
+        rows = pl.ds(816 * k, 816)
+        DD[rows, :] = jnp.dot(H[rows, :], TD[...], preferred_element_type=f32)
 
     js1 = range(-1, 5)
 
@@ -355,13 +430,7 @@
             before = carry[8 * (f - 1) : 8 * (f - 1) + 4]
             here = carry[8 * (f - 1) + 4 : 8 * f]
             after = x_blur(f, z + 3, js1)
-            w = blend(before, here, after)
-            amount = lax.rem((127 if f == 3 else 125) - 4 * z + 128, 128)
-            for j in range(4):
-                e = pltpu.roll(WF[f - 1, j], amount, 1)
-                l1 = pltpu.roll(jnp.where(last, e, w[j]), 1, 1)
-                r1 = pltpu.roll(jnp.where(first, e, w[j]), 127, 1)
-                SM[z, f - 1, j] = l1 + r1 + 2.0 * w[j]
+            put(96 * z + 32 * (f - 1), 2 + f, blend(before, here, after), z)
             new += list(here) + list(after)
         return tuple(new)
 
@@ -372,20 +441,30 @@
     for f in (1, 2, 3):
         carry += x_blur(f, 1, js1) + x_blur(f, 2, js1)
     lax.fori_loop(0, BZ // 2, field_two, tuple(carry))
+    for k in range(4):
+        rows = pl.ds(768 * k, 768)
+        SM[rows, :] = jnp.dot(H[rows, :], TF[...], preferred_element_type=f32)
 
     to_exp2 = 3.0 / (64.0 * math.log(2.0))
 
     def shade_step(z, carry):
         light, depth, red, green, blue = (list(carry[4 * k : 4 * k + 4]) for k in range(5))
         colour = [red, green, blue]
+
+        def part(plane, j, c):
+            return DD[pl.ds(pl.multiple_of(48 * (z + plane) + 8 * j, 8), 8), 128 * c : 128 * c + 128]
+
+        by = [[part(p, j, 1) for j in range(6)] for p in range(3)]
+        sy = [[part(p, j, 2) for j in range(6)] for p in range(3)]
+        along_z = blur3([b - a for a, b in zip(by[0], by[2])])
+        across = blend(*by)
+        along_y = blur3(blend(*sy))
         for j in range(4):
-            g_z = G[0, z + 2, j] - G[0, z, j]
-            g_x = G[1, z, j] + 2.0 * G[1, z + 1, j] + G[1, z + 2, j]
-            g_y = G[2, z, j] + 2.0 * G[2, z + 1, j] + G[2, z + 2, j]
+            g_z, g_x, g_y = along_z[j], across[j + 2] - across[j], along_y[j]
             facing = jnp.abs(2.0 * (g_z + g_y) + g_x)
             norm = g_z * g_z + g_x * g_x + g_y * g_y + 0.0025 * 2048.0 * 2048.0
             shading = 0.3 + 0.4 * facing * lax.rsqrt(norm)
-            grown = jnp.exp2(D[z + 1, j] * to_exp2)
+            grown = jnp.exp2(part(1, j + 1, 0) * to_exp2)
             soft = jnp.where(
                 grown < 1.0 / 128.0,
                 grown * (1.0 + grown * (-0.5 + grown * (1.0 / 3.0))),
@@ -400,7 +479,8 @@
             depth[j] = depth[j] + e
             lit = weight * shading
             for c in range(3):
-                tone = 1.0 + 0.5 * jnp.tanh(SM[z, c, j] * (1.0 / 64.0))
+                smooth = SM[pl.ds(pl.multiple_of(96 * z + 32 * c + 8 * j, 8), 8), :]
+                tone = 1.0 + 0.5 * jnp.tanh(smooth * (1.0 / 64.0))
                 colour[c][j] = colour[c][j] + lit * (LK[z, c, j] * tone)
         return tuple(light + depth + colour[0] + colour[1] + colour[2])
 
@@ -412,6 +492,8 @@
         0, BZ // 2, shade_two, tuple([jnp.ones((8, 128), f32)] * 4 + [zero] * 16)
     )
 
+    await_greetings(3)
+
     for c, k in ((0, 2), (1, 3), (2, 4), (3, 1)):
         for j in range(4):
             SB[pl.ds(8 * (j // 2) + 2 * c + j % 2, 8, stride=16), :] = final[4 * k + j]
@@ -420,7 +502,7 @@
         peer = lax.rem(gz + k, nz)
         return pltpu.make_async_remote_copy(
             src_ref=SB.at[pl.ds(pl.multiple_of(peer * 8, 8), 8)],
-            dst_ref=RB.at[pl.ds(pl.multiple_of(gz * 8, 8), 8)],
+            dst_ref=RB.at[gz],
             send_sem=a2a_send.at[k],
             recv_sem=a2a_recv.at[k],
             device_id={"gz": peer},
@@ -431,31 +513,24 @@
     for k in far_first:
         to_peer(k).start()
     own = pl.ds(pl.multiple_of(gz * 8, 8), 8)
-    RB[own, :] = SB[own, :]
+    RB[gz] = SB[own, :]
     for n, (dz, dx, dy) in enumerate(OFFSETS):
         @pl.when(there(dz, dx, dy))
         def _():
             for c in copies(n, dz, dx, dy):
                 c.wait_send()
+    for k in far_first:
+        to_peer(k).wait_send()
     for k in reversed(far_first):
         to_peer(k).wait_recv()
 
-    parts = [RB[8 * b : 8 * b + 8, :] for b in range(nz)]
-    depths = []
-    for part in parts:
+    total, image = zero, zero
+    for rank in range(nz):
+        part = RB[at_rank[rank]]
+        image = image + jnp.exp(-total) * part
         d = jnp.where(sub >= 6, part, 0.0)
         d = d + pltpu.roll(d, 4, 0)
-        depths.append(d + pltpu.roll(d, 2, 0))
-    total = depths[0]
-    for d in depths[1:]:
-        total = total + d
-    image = zero
-    for b in range(nz):
-        prior = zero
-        for o in range(nz):
-            if o != b:
-                prior = prior + jnp.where(order[o] < order[b], depths[o], 0.0)
-        image = image + jnp.exp(-prior) * parts[b]
+        total = total + (d + pltpu.roll(d, 2, 0))
     small = total * (
         1.0 + total * (-0.5 + total * (1.0 / 6.0 + total * (-1.0 / 24.0 + total * (1.0 / 120.0))))
     )
@@ -463,8 +538,6 @@
     image = jnp.where(sub >= 6, opacity, image)
     for c in range(4):
         out[c] = image[2 * c : 2 * c + 2, :]
-    for k in far_first:
-        to_peer(k).wait_send()
 
 
 def on_device(fields, material, depth_order, table):
@@ -473,7 +546,7 @@
     count = len(OFFSETS)
     return pl.pallas_call(
         kernel,
-        out_shape=jax.ShapeDtypeStruct((4, 2, 128), f32),
+        out_shape=pltpu.VMEM((4, 2, 128), f32),
         in_specs=[pl.BlockSpec(memory_space=pl.ANY)] * 4,
         out_specs=pl.BlockSpec(memory_space=pltpu.VMEM),
         scratch_shapes=[
@@ -481,23 +554,25 @@
             pltpu.VMEM((BZ, BX, 128), jnp.int32),
             vmem(2, 4, BX, 128),
             vmem(2, 4, ROWS, 128),
-            vmem(6, 8, 128),
-            vmem(2, 6, 8, 128),
-            vmem(3, 4, 8, 128),
-            vmem(3, BZ + 2, 4, 8, 128),
-            vmem(BZ + 2, 4, 8, 128),
-            vmem(BZ, 3, 4, 8, 128),
+            vmem(6, 3, 3, 16, 128),
+            pltpu.VMEM((96 * BZ, 512), bf16),
+            pltpu.VMEM((512, 384), bf16),
+            pltpu.VMEM((512, 128), bf16),
+            vmem(48 * (BZ + 2), 384),
+            vmem(96 * BZ, 128),
             vmem(BZ, 4, 4, 8, 128),
-            vmem(4, 8, 128),
-            vmem(4, 16),
+            vmem(64, 8, 128),
+            pltpu.SMEM((4, 16), f32),
+            pltpu.SMEM((16,), jnp.int32),
             pltpu.SMEM((16,), jnp.int32),
             vmem(128, 128),
-            vmem(128, 128),
+            vmem(16, 8, 128),
             dma((7,)),
             dma((count, 2)),
             dma((count, 2)),
             dma((16,)),
             dma((16,)),
+            pltpu.SemaphoreType.REGULAR((4,)),
         ],
         compiler_params=pltpu.CompilerParams(collective_id=0, has_side_effects=True),
     )(fields, material, depth_order, table)

time: 35.2 us -> 28.8 us (0.82)
  the two profiles are of different devices: /device:TPU:25 before, /device:TPU:17 now
where the time goes in v3:
time: 28.8 us; the launch traced here: 28.7 us
  Pallas kernels  28.1 us (98%)
  local copies, waits for them, and re-layouts  0.6 us (2%)
    pallas_call x1, Pallas kernels, on_device(): pl.pallas_call(kernel, out_shape=pltpu.VMEM((4, 2, 128), f32), in_specs=[...  28.1 us
    unnamed x1, local copies, waits for them, and re-layouts  0.6 us

profile of v3, /device:TPU:17, one launch (start us, length us, event | category | flops | bytes accessed | tf_op | source)
XLA Modules:
  0.0 28.7 jit_solution(8902740464606313198)
XLA Ops:
  0.0 28.1 %shard_map.46 = f32[4,2,128]{2,1,0:T(2,128)S(1)} custom-call(f32[4,32,32,128]{3,2,1,0:T(8,128)} %fields.1, s32[32,32,128]{2,1,0:T(8,128)} %material.1, s32[16]{0:T(128)} %order_hbm.1, f32[4,16]{1,0:T(4,128)} %table_hbm.1), custom_call_target="tpu_custom_call" | custom-call | tf_op jit(solution)/shard_map/pallas_call | solution.py:547
  28.1 0.6 %copy.6 = f32[4,2,128]{2,1,0:T(2,128)} copy(f32[4,2,128]{2,1,0:T(2,128)S(1)} %shard_map.46) | data formatting | bytes 8192

commit v4 on v3

--- a/solution.py
+++ b/solution.py
@@ -23,7 +23,7 @@
     for dy in (-1, 0, 1)
     if (dz, dx, dy) != (0, 0, 0)
 ]
-OFFSETS.sort(key=lambda o: -abs(o[0]) - abs(o[1]) - abs(o[2]))
+OFFSETS.sort(key=lambda o: (o[2] == 0, -abs(o[0]) - abs(o[1]) - abs(o[2])))
 
 
 def z_range(dz, width):
@@ -73,7 +73,7 @@
 
 def kernel(
     fields, material, order_hbm, table_hbm, out,
-    V, M, S, R, PE, H, TD, TF, DD, SM, LK, TB, table, order, at_rank, SB, RB,
+    V, M, S, R, PE, HD, HF, TD, TF, DD, SM, LK, TB, table, order, at_rank, SB, RB,
     load_sem, send_sem, recv_sem, a2a_send, a2a_recv, greeted,
 ):
     gz, gx, gy = lax.axis_index("gz"), lax.axis_index("gx"), lax.axis_index("gy")
@@ -97,11 +97,7 @@
     load_m = pltpu.make_async_copy(material, M, load_sem.at[4])
     load_t = pltpu.make_async_copy(table_hbm, table, load_sem.at[5])
     load_o = pltpu.make_async_copy(order_hbm, order, load_sem.at[6])
-    for c in loads:
-        c.start()
-    load_m.start()
-    load_t.start()
-    load_o.start()
+    loads[0].start()
 
     barrier = pltpu.get_barrier_semaphore()
     for dz, dx, dy in OFFSETS:
@@ -113,6 +109,12 @@
                 device_id={"gz": gz + dz, "gx": gx + dx, "gy": gy + dy},
                 device_id_type=MESH,
             )
+
+    for c in loads[1:]:
+        c.start()
+    load_m.start()
+    load_t.start()
+    load_o.start()
 
     def greet(k):
         for to in (gz + (1 << k), gz - (1 << k)):
@@ -306,14 +308,13 @@
     await_greetings(1)
     greet(2)
 
-    for n, (dz, dx, dy) in enumerate(OFFSETS):
-        @pl.when(there(-dz, -dx, -dy))
-        def _():
-            for c in copies(n, dz, dx, dy):
-                c.wait_recv()
-
-    await_greetings(2)
-    greet(3)
+    def await_cells(group):
+        for n, (dz, dx, dy) in enumerate(OFFSETS):
+            if (dz != 0) == group:
+                @pl.when(there(-dz, -dx, -dy))
+                def _():
+                    for c in copies(n, dz, dx, dy):
+                        c.wait_recv()
 
     on = lambda cond: cond.astype(f32)
     low_x = jnp.where(sub == 0, on(gx > 0), 1.0)
@@ -322,10 +323,73 @@
     def x_mask(cells):
         return [cells[0] * low_x] + cells[1:5] + [cells[5] * high_x]
 
+    js = range(-2, 6)
+    js1 = range(-1, 5)
+
+    def x_blur(f, plane, js):
+        return blur3([V[f, plane, pl.ds(ROW0 + j, 8, stride=4), :] for j in js])
+
+    def blend(a, b, c):
+        return [p + 2.0 * q + r for p, q, r in zip(a, b, c)]
+
+    def put_own(H, base, cells):
+        for p in range(len(cells) // 2):
+            rows = pl.ds(pl.multiple_of(base + 16 * p, 16), 16)
+            parts = split(jnp.concatenate([cells[2 * p], cells[2 * p + 1]], axis=0))
+            for k in range(3):
+                H[rows, 128 * k : 128 * k + 128] = parts[k]
+
+    await_cells(False)
+
+    def density_step(z, carry):
+        before, here = carry[:6], carry[6:]
+        after = x_blur(0, z + 3, js)
+        put_own(HD, 48 * z + 48, x_mask(blend(before, here, after)))
+        return tuple(here) + tuple(after)
+
+    def density_two(i, carry):
+        return density_step(2 * i + 2, density_step(2 * i + 1, carry))
+
+    lax.fori_loop(
+        0, BZ // 2 - 1, density_two, tuple(x_blur(0, 2, js)) + tuple(x_blur(0, 3, js))
+    )
+
+    def field_step(z, carry):
+        new = []
+        for f in (1, 2, 3):
+            before = carry[8 * (f - 1) : 8 * (f - 1) + 4]
+            here = carry[8 * (f - 1) + 4 : 8 * f]
+            after = x_blur(f, z + 3, js1)
+            put_own(HF, 96 * z + 32 * (f - 1), blend(before, here, after))
+            new += list(here) + list(after)
+        return tuple(new)
+
+    def field_two(i, carry):
+        return field_step(2 * i + 2, field_step(2 * i + 1, carry))
+
+    carry = []
+    for f in (1, 2, 3):
+        carry += x_blur(f, 2, js1) + x_blur(f, 3, js1)
+    lax.fori_loop(0, BZ // 2 - 1, field_two, tuple(carry))
+
+    await_cells(True)
+    await_greetings(2)
+    greet(3)
+
+    u = {p: x_blur(0, p, js) for p in (0, 1, 2, 3, 32, 33, 34, 35)}
+    put_own(HD, 0, x_mask([x * low_z for x in blend(u[0], u[1], u[2])]))
+    put_own(HD, 48, x_mask(blend(u[1], u[2], u[3])))
+    put_own(HD, 48 * BZ, x_mask(blend(u[32], u[33], u[34])))
+    put_own(HD, 48 * BZ + 48, x_mask([x * high_z for x in blend(u[33], u[34], u[35])]))
+    for f in (1, 2, 3):
+        for z in (0, BZ - 1):
+            put_own(
+                HF, 96 * z + 32 * (f - 1), blend(*[x_blur(f, z + 1 + k, js1) for k in range(3)])
+            )
+
     def packed(s, k, js):
         return [R[s, k, pl.ds(ROW0 + j, 8, stride=4), :] for j in js]
 
-    js = range(-2, 6)
     near = [packed(0, k, js) for k in range(4)]
     far = [packed(1, k, js) for k in range(4)]
     dens = [
@@ -381,69 +445,36 @@
             cells.append(below + 2.0 * main[j] + above)
         keep(2 + f, cells)
 
-    def x_blur(f, plane, js):
-        return blur3([V[f, plane, pl.ds(ROW0 + j, 8, stride=4), :] for j in js])
-
-    def blend(a, b, c):
-        return [p + 2.0 * q + r for p, q, r in zip(a, b, c)]
-
     group = lax.broadcasted_iota(jnp.int32, (16, 128), 1) // 4
 
-    def put(base, slot, cells, z):
+    def put_beside(H, base, slot, pairs, z):
         masks = [group == lax.rem(z + 11 * k, BZ) for k in range(3)]
-        for p in range(len(cells) // 2):
+        for p in range(pairs):
             rows = pl.ds(pl.multiple_of(base + 16 * p, 16), 16)
-            parts = split(jnp.concatenate([cells[2 * p], cells[2 * p + 1]], axis=0))
-            for k in range(3):
-                H[rows, 128 * k : 128 * k + 128] = parts[k]
             beside = jnp.where(masks[2], PE[slot, p, 2], 0.0)
             beside = jnp.where(masks[1], PE[slot, p, 1], beside)
             beside = jnp.where(masks[0], PE[slot, p, 0], beside)
             H[rows, 384:512] = beside.astype(bf16)
 
-    u0 = x_blur(0, 0, js)
-    u1 = x_blur(0, 1, js)
-    u2 = x_blur(0, 2, js)
-    put(0, 1, x_mask([x * low_z for x in blend(u0, u1, u2)]), 0)
-
-    def density_step(z, carry):
-        before, here = carry[:6], carry[6:]
-        after = x_blur(0, z + 3, js)
-        put(48 * z + 48, 0, x_mask(blend(before, here, after)), z)
-        return tuple(here) + tuple(after)
-
-    def density_two(i, carry):
-        return density_step(2 * i + 1, density_step(2 * i, carry))
-
-    carry = lax.fori_loop(0, BZ // 2, density_two, tuple(u1) + tuple(u2))
-    u3 = x_blur(0, BZ + 3, js)
-    put(48 * BZ + 48, 2, x_mask([x * high_z for x in blend(carry[:6], carry[6:], u3)]), BZ - 1)
+    put_beside(HD, 0, 1, 3, 0)
+    put_beside(HD, 48 * BZ + 48, 2, 3, BZ - 1)
+
+    def beside_step(z):
+        put_beside(HD, 48 * z + 48, 0, 3, z)
+        for f in (1, 2, 3):
+            put_beside(HF, 96 * z + 32 * (f - 1), 2 + f, 2, z)
+
+    @pl.loop(0, BZ // 2)
+    def _(i):
+        beside_step(2 * i)
+        beside_step(2 * i + 1)
+
     for k in range(2):
         rows = pl.ds(816 * k, 816)
-        DD[rows, :] = jnp.dot(H[rows, :], TD[...], preferred_element_type=f32)
-
-    js1 = range(-1, 5)
-
-    def field_step(z, carry):
-        new = []
-        for f in (1, 2, 3):
-            before = carry[8 * (f - 1) : 8 * (f - 1) + 4]
-            here = carry[8 * (f - 1) + 4 : 8 * f]
-            after = x_blur(f, z + 3, js1)
-            put(96 * z + 32 * (f - 1), 2 + f, blend(before, here, after), z)
-            new += list(here) + list(after)
-        return tuple(new)
-
-    def field_two(i, carry):
-        return field_step(2 * i + 1, field_step(2 * i, carry))
-
-    carry = []
-    for f in (1, 2, 3):
-        carry += x_blur(f, 1, js1) + x_blur(f, 2, js1)
-    lax.fori_loop(0, BZ // 2, field_two, tuple(carry))
+        DD[rows, :] = jnp.dot(HD[rows, :], TD[...], preferred_element_type=f32)
     for k in range(4):
         rows = pl.ds(768 * k, 768)
-        SM[rows, :] = jnp.dot(H[rows, :], TF[...], preferred_element_type=f32)
+        SM[rows, :] = jnp.dot(HF[rows, :], TF[...], preferred_element_type=f32)
 
     to_exp2 = 3.0 / (64.0 * math.log(2.0))
 
@@ -555,6 +586,7 @@
             vmem(2, 4, BX, 128),
             vmem(2, 4, ROWS, 128),
             vmem(6, 3, 3, 16, 128),
+            pltpu.VMEM((48 * (BZ + 2), 512), bf16),
             pltpu.VMEM((96 * BZ, 512), bf16),
             pltpu.VMEM((512, 384), bf16),
             pltpu.VMEM((512, 128), bf16),

time: 28.8 us -> 28.7 us (level)
  no operation moved by 1% of the time
where the time goes in v4:
time: 28.7 us; the launch traced here: 28.5 us
  Pallas kernels  27.9 us (97%)
  local copies, waits for them, and re-layouts  0.6 us (2%)
    pallas_call x1, Pallas kernels, on_device(): pl.pallas_call(kernel, out_shape=pltpu.VMEM((4, 2, 128), f32), in_specs=[...  27.9 us
    unnamed x1, local copies, waits for them, and re-layouts  0.6 us

profile of v4, /device:TPU:17, one launch (start us, length us, event | category | flops | bytes accessed | tf_op | source)
XLA Modules:
  0.0 28.5 jit_solution(16148389445141895303)
XLA Ops:
  0.0 27.9 %shard_map.46 = f32[4,2,128]{2,1,0:T(2,128)S(1)} custom-call(f32[4,32,32,128]{3,2,1,0:T(8,128)} %fields.1, s32[32,32,128]{2,1,0:T(8,128)} %material.1, s32[16]{0:T(128)} %order_hbm.1, f32[4,16]{1,0:T(4,128)} %table_hbm.1), custom_call_target="tpu_custom_call" | custom-call | tf_op jit(solution)/shard_map/pallas_call | solution.py:578
  27.9 0.6 %copy.6 = f32[4,2,128]{2,1,0:T(2,128)} copy(f32[4,2,128]{2,1,0:T(2,128)S(1)} %shard_map.46) | data formatting | bytes 8192

commit v5 on v4

--- a/solution.py
+++ b/solution.py
@@ -515,12 +515,14 @@
                 colour[c][j] = colour[c][j] + lit * (LK[z, c, j] * tone)
         return tuple(light + depth + colour[0] + colour[1] + colour[2])
 
-    def shade_two(i, carry):
-        return shade_step(2 * i + 1, shade_step(2 * i, carry))
+    def shade_four(i, carry):
+        for k in range(4):
+            carry = shade_step(4 * i + k, carry)
+        return carry
 
     zero = jnp.zeros((8, 128), f32)
     final = lax.fori_loop(
-        0, BZ // 2, shade_two, tuple([jnp.ones((8, 128), f32)] * 4 + [zero] * 16)
+        0, BZ // 4, shade_four, tuple([jnp.ones((8, 128), f32)] * 4 + [zero] * 16)
     )
 
     await_greetings(3)

time: 28.7 us -> 28.6 us (level)
  no operation moved by 1% of the time
where the time goes in v5:
time: 28.6 us; the launch traced here: 28.4 us
  Pallas kernels  27.8 us (97%)
  local copies, waits for them, and re-layouts  0.6 us (2%)
    pallas_call x1, Pallas kernels, on_device(): pl.pallas_call(kernel, out_shape=pltpu.VMEM((4, 2, 128), f32), in_specs=[...  27.8 us
    unnamed x1, local copies, waits for them, and re-layouts  0.6 us

profile of v5, /device:TPU:17, one launch (start us, length us, event | category | flops | bytes accessed | tf_op | source)
XLA Modules:
  0.0 28.4 jit_solution(8621682953813948604)
XLA Ops:
  0.0 27.8 %shard_map.46 = f32[4,2,128]{2,1,0:T(2,128)S(1)} custom-call(f32[4,32,32,128]{3,2,1,0:T(8,128)} %fields.1, s32[32,32,128]{2,1,0:T(8,128)} %material.1, s32[16]{0:T(128)} %order_hbm.1, f32[4,16]{1,0:T(4,128)} %table_hbm.1), custom_call_target="tpu_custom_call" | custom-call | tf_op jit(solution)/shard_map/pallas_call | solution.py:580
  27.8 0.6 %copy.6 = f32[4,2,128]{2,1,0:T(2,128)} copy(f32[4,2,128]{2,1,0:T(2,128)S(1)} %shard_map.46) | data formatting | bytes 8192
